TPU v7x, 256 devices: a whole 4x4x8 slice. The times are simulated.
256 devices in a mesh: dp: 4 (over x), psg: 64 (over y, z, core).
Axes of the slice: x: 4, y: 4, z: 8, core: 2. Of those that a mesh axis runs over, the one named last changes fastest.
Arguments:
- queries: bfloat16 [4, 128, 2048], P('dp', None, 'psg'), may hold values from -4 to 4
- keys: bfloat16 [4, 128, 256, 2048], P('dp', 'psg'), may hold values from -4 to 4
- values: bfloat16 [4, 128, 256, 2048], P('dp', 'psg'), may hold values from -6 to 6
- lengths: int32 [4, 128], P('dp', 'psg'), may hold values from 16 to 256, as said below
- out_weight: bfloat16 [4096, 2048], P('psg'), may hold values from -0.125 to 0.125
- out_cotangent: bfloat16 [4, 128, 4096], P('dp', None, 'psg'), may hold values from -6 to 6
Outputs:
- layer_out: bfloat16 [4, 128, 4096], P('dp', None, 'psg')
- weight_grad: float32 [4096, 2048], P('psg')
- query_grad: bfloat16 [4, 128, 2048], P('dp', None, 'psg')
- key_grad: bfloat16 [4, 128, 256, 2048], P('dp', 'psg')
- value_grad: bfloat16 [4, 128, 256, 2048], P('dp', 'psg')
Inputs may be any that keep to these rules, and one draw needn't show every extreme that they name: `lengths`: every passage has at least 16 valid tokens, counted from its start; in every question some passage has all 256.
All inputs are finite; a program needn't handle non-finite values.
Results may differ from a plain program's by a relative error of at most 0.025.
Values may be sent and summed in bfloat16 or wider, within the bound.
A program may use at most 64 MiB of HBM per device.

v0:
```python
import jax
import jax.numpy as jnp
from jax import lax
from jax.sharding import PartitionSpec as P

HEAD_COUNT = 32
HEAD_SIZE = 64


def spread_heads(factor):
    return jnp.transpose(factor, (0, 2, 1))[..., None]


def local_weights(scores, valid_keys, row_max):
    return jnp.where(valid_keys, jnp.exp(scores - row_max[..., None]), 0.0)


def weighted_values(weights, value_heads):
    output = jnp.einsum(
        "bhik,bkhe->bihe",
        weights.astype(jnp.bfloat16),
        value_heads,
        preferred_element_type=jnp.float32,
    )
    return output.reshape(output.shape[0], output.shape[1], -1)


def per_device(queries, keys, values, lengths, out_weight, out_cotangent):
    question_count = keys.shape[0]
    key_count = keys.shape[1] * keys.shape[2]
    inner_dim = keys.shape[3]
    answer_len = queries.shape[1]
    head_split = (question_count, answer_len, HEAD_COUNT, HEAD_SIZE)
    query_full = lax.all_gather(queries, "psg", axis=2, tiled=True)
    query_heads = query_full.reshape(head_split)
    key_heads = keys.reshape(question_count, key_count, HEAD_COUNT, HEAD_SIZE)
    value_heads = values.reshape(question_count, key_count, HEAD_COUNT, HEAD_SIZE)
    positions = jnp.arange(keys.shape[2], dtype=jnp.int32)
    valid_keys = (positions[None, None, :] < lengths[:, :, None]).reshape(
        question_count, 1, 1, key_count
    )
    scores = jnp.einsum(
        "bihe,bkhe->bhik", query_heads, key_heads, preferred_element_type=jnp.float32
    )
    local_max = jnp.max(jnp.where(valid_keys, scores, -jnp.inf), axis=3)
    row_max = lax.pmax(local_max, "psg")
    weights = local_weights(scores, valid_keys, row_max)
    row_sum, output = lax.psum(
        (jnp.sum(weights, axis=3), weighted_values(weights, value_heads)), "psg"
    )
    context = (
        (output.reshape(head_split) / spread_heads(row_sum))
        .astype(jnp.bfloat16)
        .reshape(question_count, answer_len, inner_dim)
    )
    context_rows = context.reshape(question_count * answer_len, inner_dim)
    grad_rows = out_cotangent.reshape(question_count * answer_len, -1)
    layer_out = jnp.dot(context_rows, out_weight.T, preferred_element_type=jnp.float32).astype(
        jnp.bfloat16
    )
    layer_out = layer_out.reshape(question_count, answer_len, -1)
    weight_grad = lax.psum(
        jnp.dot(grad_rows.T, context_rows, preferred_element_type=jnp.float32).astype(jnp.bfloat16),
        "dp",
    ).astype(jnp.float32)
    context_grad = lax.psum(
        jnp.dot(grad_rows, out_weight, preferred_element_type=jnp.float32), "psg"
    ).astype(jnp.bfloat16)
    grad_heads = context_grad.reshape(head_split)
    products = context_grad.reshape(question_count, answer_len, inner_dim).astype(
        jnp.float32
    ) * context.astype(jnp.float32)
    row_dots = jnp.transpose(jnp.sum(products.reshape(head_split), axis=3), (0, 2, 1))
    probs = weights / row_sum[..., None]
    prob_grad = jnp.einsum(
        "bihe,bkhe->bhik", grad_heads, value_heads, preferred_element_type=jnp.float32
    )
    score_grad = (probs * (prob_grad - row_dots[..., None])).astype(jnp.bfloat16)
    value_grad = jnp.einsum(
        "bhik,bihe->bkhe",
        probs.astype(jnp.bfloat16),
        grad_heads,
        preferred_element_type=jnp.float32,
    )
    value_grad = value_grad.astype(jnp.bfloat16).reshape(values.shape)
    key_grad = jnp.einsum(
        "bhik,bihe->bkhe", score_grad, query_heads, preferred_element_type=jnp.float32
    )
    key_grad = key_grad.astype(jnp.bfloat16).reshape(keys.shape)
    query_terms = jnp.einsum(
        "bhik,bkhe->bihe", score_grad, key_heads, preferred_element_type=jnp.float32
    )
    query_terms = query_terms.reshape(question_count, answer_len, inner_dim)
    query_grad = lax.psum_scatter(query_terms, "psg", scatter_dimension=2, tiled=True).astype(
        jnp.bfloat16
    )
    return (layer_out, weight_grad, query_grad, key_grad, value_grad)


def solution(mesh):
    return jax.shard_map(
        per_device,
        mesh=mesh,
        in_specs=(
            P("dp", None, "psg"),
            P("dp", "psg", None, None),
            P("dp", "psg", None, None),
            P("dp", "psg"),
            P("psg", None),
            P("dp", None, "psg"),
        ),
        out_specs=(
            P("dp", None, "psg"),
            P("psg", None),
            P("dp", None, "psg"),
            P("dp", "psg", None, None),
            P("dp", "psg", None, None),
        ),
        check_vma=False,
    )
```

profile of v0, /device:TPU:1, one launch (start us, length us, event | category | flops | bytes accessed | tf_op | source)
XLA Modules:
  0.0 801.0 jit_solution(5263809331507531517)
XLA Ops:
  7.2 0.0 copy-start
  7.2 0.0 all-reduce.5.cloned.1.call-start
  7.2 54.9 %all_gather.3 = bf16[1,128,2048]{1,2,0:T(8,128)(2,1)S(1)} all-gather(bf16[1,128,32]{1,2,0:T(8,128)(2,1)} %param.6), channel_id=1, replica_groups=mesh['dp'=4,'psg'=64] {'psg'}, dimensions={2}, use_global_device_ids=true | all-gather | bytes 532480 | tf_op jit(solution)/shard_map/all_gather | solution.py:34
  62.2 0.0 copy-start.2
  62.2 0.0 copy-start.8
  62.2 6.3 copy.21
  68.5 3.2 reshape.146
  71.7 0.0 copy-done.8
  71.7 0.1 lt.25
  71.8 0.0 copy-done.2
  71.8 4.5 select_reduce_fusion
  76.3 243.2 %pmax.7 = f32[32,128]{1,0:T(8,128)S(1)} all-reduce(f32[32,128]{1,0:T(8,128)S(1)} %get-tuple-element.19), channel_id=1, replica_groups=mesh['dp'=4,'psg'=64] {'psg'}, use_global_device_ids=true, to_apply=%region_1.2 | all-reduce | flops 4096 | bytes 32768 | tf_op jit(solution)/shard_map/pmax | solution.py:46
  319.5 6.1 copy.22
  325.7 4.4 reshape.147
  330.0 0.0 copy-start.7
  330.0 5.7 fusion.3
  335.7 1.3 copy.23
  337.0 0.0 all-reduce.5.cloned.1.call-update
  337.1 0.0 all-reduce.7.cloned.1.call-start
  337.1 0.0 copy-done
  337.1 0.0 copy-done.7
  337.1 0.3 fusion.17
  337.5 4.6 fusion.1
  342.0 259.0 %all-reduce.8 = (f32[1,32,128]{2,1,0:T(8,128)S(1)}, bf16[128,2048]{1,0:T(8,128)(2,1)}) all-reduce(f32[1,32,128]{2,1,0:T(8,128)S(1)} %bitcast.95, f32[128,2048]{1,0:T(8,128)S(1)} %fusion.17), channel_id=1, replica_groups=mesh['dp'=4,'psg'=64] {'psg'}, use_global_device_ids=true, to_apply=%region_4.5 | all-reduce | flops 266240 | bytes 1605632 | tf_op jit(solution)/shard_map/psum | solution.py:48
  601.1 0.1 div.33
  601.1 1.3 copy.24
  602.4 1.3 copy.25
  603.7 0.0 copy-start.4
  603.7 2.1 copy.26
  605.9 0.0 all-reduce.5.cloned.1.call-done
  605.9 2.6 fusion.10
  608.4 0.0 all-reduce.7.cloned.1.call-update
  608.5 0.2 reduce-scatter.2.cloned.1.call-start
  608.7 0.0 copy-done.4
  608.7 2.8 convert_multiply_fusion
  611.4 1.5 copy.27
  613.0 0.1 bitcast_reduce_fusion
  613.1 5.8 multiply_convert_fusion
  618.9 0.0 copy-start.1
  618.9 0.0 copy-start.6
  618.9 2.6 fusion.23
  621.5 0.0 copy-done.1
  621.5 0.0 reduce-scatter.2.cloned.1.call-update
  621.5 0.0 copy-done.6
  621.5 5.7 convert_bitcast_fusion
  627.3 0.0 copy-start.3
  627.3 2.6 reshape.156
  629.9 4.6 copy.29
  634.5 0.0 copy-done.3
  634.5 2.9 convert_bitcast_fusion.1
  637.4 0.0 copy-start.5
  637.4 2.1 reshape.155
  639.5 6.1 copy.28
  645.6 0.0 copy-done.5
  645.6 0.9 fusion.14
  646.5 5.7 all-reduce.7.cloned.1.call-done
  652.2 1.8 convert_element_type.78
  654.0 139.2 %reduce-scatter.2.cloned.1.call-done = f32[1,128,32]{1,2,0:T(8,128)} async-done(((f32[1,128,2048]{1,2,0:T(8,128)}), f32[1,128,32]{1,2,0:T(8,128)}) %reduce-scatter.2.cloned.1.call-update) | async-done | bytes 16400 | tf_op jit(solution)/shard_map/reduce_scatter | solution.py:94
  793.2 1.3 convert_element_type.83
  (3 shorter events, 0.0 us)
Async XLA Ops:
  7.2 329.9 %copy-start = (bf16[64,2048]{1,0:T(8,128)(2,1)S(1)}, bf16[64,2048]{1,0:T(8,128)(2,1)}, u32[]{:S(2)}) copy-start(bf16[64,2048]{1,0:T(8,128)(2,1)} %param.10) | copy-start | bytes 786436
  7.2 598.7 %all-reduce.5.cloned.1.call-start = ((), (), s32[]{:S(2)}) async-start(), calls=%async_computation.1 | async-start | bytes 2097152 | tf_op jit(solution)/shard_map/psum | solution.py:48
  62.2 9.6 %copy-start.2 = (bf16[1,128,2048]{1,2,0:T(8,128)(2,1)}, bf16[1,128,2048]{1,2,0:T(8,128)(2,1)S(1)}, u32[]{:S(2)}) copy-start(bf16[1,128,2048]{1,2,0:T(8,128)(2,1)S(1)} %all_gather.3) | copy-start | bytes 1572868
  62.2 9.5 %copy-start.8 = (s32[1,2]{1,0:T(1,128)S(1)}, s32[1,2]{1,0:T(1,128)}, u32[]{:S(2)}) copy-start(s32[1,2]{1,0:T(1,128)} %param.9) | copy-start | bytes 28
  330.0 7.1 copy-start.7
  337.1 315.1 %all-reduce.7.cloned.1.call-start = ((), (), s32[]{:S(2)}) async-start(), calls=%async_computation.2 | async-start | bytes 524288 | tf_op jit(solution)/shard_map/psum | solution.py:62
  603.7 4.9 copy-start.4
  608.5 184.7 %reduce-scatter.2.cloned.1.call-start = ((), (), s32[]{:S(2)}) async-start(), calls=%async_computation.3 | async-start | bytes 1064960 | tf_op jit(solution)/shard_map/reduce_scatter | solution.py:94
  618.9 2.6 copy-start.1
  618.9 2.6 copy-start.6
  627.3 7.2 copy-start.3
  637.4 8.3 %copy-start.5 = (bf16[128,2048]{1,0:T(8,128)(2,1)S(1)}, bf16[128,2048]{1,0:T(8,128)(2,1)}, u32[]{:S(2)}) copy-start(bf16[128,2048]{1,0:T(8,128)(2,1)} %get-tuple-element.18) | copy-start | bytes 1572868
Sparse Core Ops, SparseCore 0:
  337.2 183.2 all-reduce.4
  608.6 43.5 all-reduce.6
  656.2 136.9 reduce-scatter.1
where the time goes:
time: 806 us; the launch traced here: 801 us
  blocking collectives  557 us (69%)
  waiting for transfers between devices  145 us (18%)
  local copies, waits for them, and re-layouts  43.2 us (5%)
  matrix products  31 us (4%)
  between operations  13.9 us (2%)
  other arithmetic  10.5 us (1%)
    psum x1, blocking collectives, per_device(): lax.psum((jnp.sum(weights, axis=3), weighted_values(weights, value_heads)...  259 us
    pmax x1, blocking collectives, per_device(): row_max = lax.pmax(local_max, 'psg')  243 us
    reduce_scatter x1, waiting for transfers between devices, per_device(): lax.psum_scatter(query_terms, 'psg', scatter_dimension=2, tiled=True)  139 us
    all_gather x1, blocking collectives, per_device(): query_full = lax.all_gather(queries, 'psg', axis=2, tiled=True)  54.9 us
    unnamed x24, local copies, waits for them, and re-layouts  23.2 us
  transfers between devices with their start and end apart: 3, of which 2 were waited for; matrix products, arithmetic and copies ran while one was open for 6% of the time, Pallas kernels for 0%

commit v1 on v0

v1 whole, which is shorter than its diff:
```python
import functools

import jax
import jax.numpy as jnp
from jax import lax
from jax.experimental import pallas as pl
from jax.experimental.pallas import tpu as pltpu
from jax.sharding import PartitionSpec as P

BF = jnp.bfloat16
F32 = jnp.float32
MESH = pl.DeviceIdType.MESH
MASKED = -1e30
GRIDS = {64: (4, 8), 8: (2, 2)}

NN = (((1,), (0,)), ((), ()))
NT = (((1,), (1,)), ((), ()))
TN = (((0,), (0,)), ((), ()))


def dot(a, b, dims=NN):
    return lax.dot_general(a, b, dims, preferred_element_type=F32)


def eye(n):
    rows = lax.broadcasted_iota(jnp.int32, (n, n), 0)
    cols = lax.broadcasted_iota(jnp.int32, (n, n), 1)
    return jnp.where(rows == cols, 1.0, 0.0).astype(BF)


def block_diagonal(pair):
    zero = jnp.zeros((64, pair.shape[1]), pair.dtype)
    first = jnp.concatenate([pair[:64], zero], axis=0)
    second = jnp.concatenate([zero, pair[64:]], axis=0)
    return jnp.concatenate([first, second], axis=1)


class Wires:
    def __init__(self, send_sems, recv_sems):
        self.send_sems, self.recv_sems = send_sems, recv_sems
        self.count = 0
        self.sent = []

    def send(self, src, dst, device_id):
        copy = pltpu.make_async_remote_copy(
            src_ref=src,
            dst_ref=dst,
            send_sem=self.send_sems.at[self.count],
            recv_sem=self.recv_sems.at[self.count],
            device_id=device_id,
            device_id_type=MESH,
        )
        self.count += 1
        copy.start()
        self.sent.append(copy)
        return copy

    def finish(self):
        for copy in self.sent:
            copy.wait_send()


def layer_kernel(
    dims,
    q_ref, k_hbm, v_hbm, len_ref, w_ref, g_ref,
    lo_ref, wg_ref, dq_ref, dk_hbm, dv_hbm,
    kb, vb, dkb, dvb, pb, bias,
    qb, gb, cb, fgb, dots,
    po, st, rco, rcs, tbo, tbs, ryo, rys, tzo, tzs, rzo, rzs, sg,
    pg, rcg, tbg, ryg, tzg, rzg,
    pd, rcd, tbd, ryd, tzd, rzd,
    wgp, rxw, wgf,
    send_sems, recv_sems, load_sems, store_sems,
):
    X, Y, Z, tokens = dims
    heads = Y * Z
    keys = kb.shape[0]
    width = Z * 64
    x = lax.axis_index("dp")
    me = lax.axis_index("psg")
    c = lax.rem(me, 2)
    chip = me // 2
    z = lax.rem(chip, Z)
    y = chip // Z

    def at_z(k):
        return {"psg": (y * Z + lax.rem(z + k, Z)) * 2 + c}

    def at_y(k):
        return {"psg": (lax.rem(y + k, Y) * Z + z) * 2 + c}

    def at_x(k):
        return {"dp": lax.rem(x + k, X)}

    partner = {"psg": chip * 2 + (1 - c)}
    wires = Wires(send_sems, recv_sems)

    def block_of(k):
        return lax.rem(y + k, Y)

    def rows(b):
        return pl.ds(b * Z, Z)

    def lanes(b):
        return pl.ds(pl.multiple_of(b * width, width), width)

    loads = []
    for i in range(Y):
        b = block_of(i + 1)
        pair = []
        for n, (src, dst) in enumerate(((k_hbm, kb), (v_hbm, vb))):
            copy = pltpu.make_async_copy(
                src.at[:, lanes(b)], dst.at[:, lanes(b)], load_sems.at[2 * i + n]
            )
            copy.start()
            pair.append(copy)
        loads.append(pair)

    barrier = pltpu.get_barrier_semaphore()
    peers = [partner]
    peers += [at_z(k) for k in range(1, Z)]
    peers += [at_y(k) for k in range(1, Y)]
    peers += [at_x(k) for k in range(1, X)]
    for peer in peers:
        pl.semaphore_signal(barrier, inc=1, device_id=peer, device_id_type=MESH)

    qb[chip, c] = dot(eye(32), q_ref[...], NT).astype(BF)
    g_t = dot(eye(64), g_ref[...], NT).astype(BF)
    pl.semaphore_wait(barrier, len(peers))

    def gather_z(buf):
        return [wires.send(buf.at[chip, c], buf.at[chip, c], at_z(k)) for k in range(1, Z)]

    def gather_y(buf, z_copies):
        for copy in z_copies:
            copy.wait_recv()
        own = buf.at[rows(y), c]
        y_copies = [wires.send(own, own, at_y(k)) for k in range(1, Y)]
        return y_copies, [wires.send(own, own, partner)]

    def gather_core(buf, y_copies, core_copies):
        core_copies = list(core_copies)
        for k in range(1, Y):
            y_copies[k - 1].wait_recv()
            part = buf.at[rows(block_of(Y - k)), c]
            core_copies.append(wires.send(part, part, partner))
        return core_copies

    def gather_end(core_copies):
        for copy in core_copies:
            copy.wait_recv()

    def scatter_core(part, landing, b):
        return wires.send(part.at[rows(b), 1 - c], landing.at[rows(b)], partner)

    def scatter_y(part, landing, total, landing_y, copy, b, k):
        copy.wait_recv()
        both = part[rows(b), c].astype(F32) + landing[rows(b)].astype(F32)
        total[rows(b)] = both.astype(BF)
        if k < Y:
            return wires.send(total.at[rows(b)], landing_y.at[k - 1], at_y(k))
        return None

    def scatter_z(total, landing_y, total_z, landing_z, copies):
        both = total[rows(y)].astype(F32)
        for k in range(1, Y):
            copies[k - 1].wait_recv()
            both = both + landing_y[k - 1].astype(F32)
        total_z[...] = both.astype(BF)
        return [
            wires.send(total_z.at[lax.rem(z + k, Z)], landing_z.at[k - 1], at_z(k))
            for k in range(1, Z)
        ]

    def scatter_end(total_z, landing_z, copies):
        both = total_z[z].astype(F32)
        for k in range(1, Z):
            copies[k - 1].wait_recv()
            both = both + landing_z[k - 1].astype(F32)
        return both

    q_z = gather_z(qb)
    g_core = []
    for i in range(Y):
        b = block_of(i + 1)
        term = dot(w_ref[:, lanes(b)], g_t, TN)
        pg[rows(b)] = term.reshape(Z, 2, 32, term.shape[1]).astype(BF)
        g_core.append(scatter_core(pg, rcg, b))
    q_y, q_core = gather_y(qb, q_z)
    g_y = []
    for i in range(Y):
        g_y.append(scatter_y(pg, rcg, tbg, ryg, g_core[i], block_of(i + 1), i + 1))

    for passage in range(keys // tokens):
        position = lax.broadcasted_iota(jnp.int32, (tokens, bias.shape[1]), 0)
        bias[passage * tokens : (passage + 1) * tokens] = jnp.where(
            position < len_ref[0, passage], 0.0, MASKED
        )
    q_core = gather_core(qb, q_y, q_core)
    g_z = scatter_z(tbg, ryg, tzg, rzg, g_y)
    gather_end(q_core)

    def forward_pair(j):
        columns = pl.ds(pl.multiple_of(j * 128, 128), 128)
        answers = qb.shape[3]
        query = block_diagonal(qb[pl.ds(2 * j, 2)].reshape(128, answers))
        scores = dot(kb[:, columns], query)
        for half in range(2):
            part = scores[:, half * answers : (half + 1) * answers] + bias[...]
            top = jnp.max(part, axis=0, keepdims=True)
            weights = jnp.exp(part - top)
            st[2 * j + half, 0:1, :] = top
            st[2 * j + half, 1:2, :] = jnp.sum(weights, axis=0, keepdims=True)
            pb[j, :, half * answers : (half + 1) * answers] = weights.astype(BF)
        out = dot(vb[:, columns], pb[j], TN)
        po[2 * j] = out[:64, :answers].reshape(2, 32, answers).astype(BF)
        po[2 * j + 1] = out[64:, answers:].reshape(2, 32, answers).astype(BF)

    def run_block(body, b):
        @pl.loop(0, Z // 2)
        def _(i):
            body(b * (Z // 2) + i)

    def merge(terms):
        top = terms[0][1]
        for _, other, _ in terms[1:]:
            top = jnp.maximum(top, other)
        output, total = None, None
        for out, own, part in terms:
            scale = jnp.exp(own - top)
            output = out * scale if output is None else output + out * scale
            total = part * scale if total is None else total + part * scale
        return output, top, total

    def triple(out, stats):
        return out.astype(F32), stats[..., 0:1, :], stats[..., 1:2, :]

    def output_core(b):
        return scatter_core(po, rco, b), wires.send(st.at[rows(b)], rcs.at[rows(b)], partner)

    def output_y(copies, b, k):
        for copy in copies:
            copy.wait_recv()
        output, top, total = merge(
            [triple(po[rows(b), c], st[rows(b)]), triple(rco[rows(b)], rcs[rows(b)])]
        )
        tbo[rows(b)] = output.astype(BF)
        tbs[rows(b), 0:1, :] = top
        tbs[rows(b), 1:2, :] = total
        if k == Y:
            return None
        return (
            wires.send(tbo.at[rows(b)], ryo.at[k - 1], at_y(k)),
            wires.send(tbs.at[rows(b)], rys.at[k - 1], at_y(k)),
        )

    o_core, o_y = [], []
    for i in range(Y):
        b = block_of(i + 1)
        for copy in loads[i]:
            copy.wait()
        run_block(forward_pair, b)
        o_core.append(output_core(b))
        if i > 0:
            o_y.append(output_y(o_core[i - 1], block_of(i), i))
        if i == 0:
            gb[chip, c] = scatter_end(tzg, rzg, g_z).astype(BF)
            gg_z = gather_z(gb)
        if i == 1:
            gg_y, gg_core = gather_y(gb, gg_z)
    output_y(o_core[Y - 1], y, Y)
    gg_core = gather_core(gb, gg_y, gg_core)

    terms = [triple(tbo[rows(y)], tbs[rows(y)])]
    for k in range(1, Y):
        for copy in o_y[k - 1]:
            copy.wait_recv()
        terms.append(triple(ryo[k - 1], rys[k - 1]))
    output, top, total = merge(terms)
    tzo[...] = output.astype(BF)
    tzs[:, 0:1, :] = top
    tzs[:, 1:2, :] = total
    o_z = []
    for k in range(1, Z):
        t = lax.rem(z + k, Z)
        o_z.append(
            (
                wires.send(tzo.at[t], rzo.at[k - 1], at_z(k)),
                wires.send(tzs.at[t], rzs.at[k - 1], at_z(k)),
            )
        )
    terms = [triple(tzo[z], tzs[z])]
    for k in range(1, Z):
        for copy in o_z[k - 1]:
            copy.wait_recv()
        terms.append(triple(rzo[k - 1], rzs[k - 1]))
    output, top, total = merge(terms)
    context = (output / total).astype(BF)
    cb[chip, c] = context
    sg[chip, c, 0:1, :] = top
    sg[chip, c, 1:2, :] = total
    sg[chip, c, 2:3, :] = jnp.sum(
        gb[chip, c].astype(F32) * context.astype(F32), axis=0, keepdims=True
    )
    sg[chip, c, 3:4, :] = total

    s_z = gather_z(sg)
    c_z = gather_z(cb)
    s_y, s_core = gather_y(sg, s_z)
    c_y, c_core = gather_y(cb, c_z)
    s_core = gather_core(sg, s_y, s_core)
    gather_end(gg_core)
    gather_end(s_core)

    for b in range(Y):
        part = slice(b * Z, (b + 1) * Z)
        factor = jnp.exp(st[part, 0:1, :] - sg[part, 0, 0:1, :]) / sg[part, 0, 1:2, :]
        dots[part] = factor * (sg[part, 0, 2:3, :] + sg[part, 1, 2:3, :])
        grads = gb[part].astype(F32).reshape(Z, 64, gb.shape[3]) * factor
        fgb[part] = grads.astype(BF).reshape(Z, 2, 32, gb.shape[3])

    def backward_pair(j):
        columns = pl.ds(pl.multiple_of(j * 128, 128), 128)
        answers = qb.shape[3]
        query = block_diagonal(qb[pl.ds(2 * j, 2)].reshape(128, answers))
        grad = block_diagonal(fgb[pl.ds(2 * j, 2)].reshape(128, answers))
        row_dots = jnp.concatenate([dots[2 * j], dots[2 * j + 1]], axis=1)
        weight_grad = dot(vb[:, columns], grad)
        weights = pb[j]
        score_grad = (weights.astype(F32) * (weight_grad - row_dots)).astype(BF)
        dvb[:, columns] = dot(weights, grad, NT).astype(BF)
        dkb[:, columns] = dot(score_grad, query, NT).astype(BF)
        out = dot(kb[:, columns], score_grad, TN)
        pd[2 * j] = out[:64, :answers].reshape(2, 32, answers).astype(BF)
        pd[2 * j + 1] = out[64:, answers:].reshape(2, 32, answers).astype(BF)

    d_core, d_y, stores = [], [], []
    for i in range(Y):
        b = block_of(i + 1)
        run_block(backward_pair, b)
        d_core.append(scatter_core(pd, rcd, b))
        for n, (src, dst) in enumerate(((dkb, dk_hbm), (dvb, dv_hbm))):
            copy = pltpu.make_async_copy(
                src.at[:, lanes(b)], dst.at[:, lanes(b)], store_sems.at[2 * i + n]
            )
            copy.start()
            stores.append(copy)
        if i > 0:
            d_y.append(scatter_y(pd, rcd, tbd, ryd, d_core[i - 1], block_of(i), i))
        if i == 0:
            c_core = gather_core(cb, c_y, c_core)
        if i == 1:
            gather_end(c_core)
            everything = cb[...].reshape(heads * 64, cb.shape[3])
            out_t = dot(w_ref[...], everything).astype(BF)
            lo_ref[...] = dot(eye(out_t.shape[1]), out_t, NT).astype(BF)
            span = heads * 64 // X
            for n in range(X):
                wgp[n] = dot(g_t, everything[n * span : (n + 1) * span], NT).astype(BF)
            w_copies = [
                wires.send(wgp.at[lax.rem(x + k, X)], rxw.at[k - 1], at_x(k)) for k in range(1, X)
            ]
        if i == min(2, Y - 1):
            both = wgp[x].astype(F32)
            for k in range(1, X):
                w_copies[k - 1].wait_recv()
                both = both + rxw[k - 1].astype(F32)
            wgf[x] = both.astype(BF)
            w_copies = [wires.send(wgf.at[x], wgf.at[x], at_x(k)) for k in range(1, X)]
    scatter_y(pd, rcd, tbd, ryd, d_core[Y - 1], y, Y)
    d_z = scatter_z(tbd, ryd, tzd, rzd, d_y)
    for copy in w_copies:
        copy.wait_recv()
    span = heads * 64 // X
    for n in range(X):
        wg_ref[:, n * span : (n + 1) * span] = wgf[n]
    own = scatter_end(tzd, rzd, d_z).astype(BF)
    dq_ref[...] = dot(eye(own.shape[1]), own, NT).astype(BF)

    for copy in stores:
        copy.wait()
    wires.finish()


def per_device(grid, chips_x, queries, keys, values, lengths, out_weight, out_cotangent):
    Y, Z = grid
    X = chips_x
    answers = queries.shape[1]
    tokens = keys.shape[2]
    count = keys.shape[1] * tokens
    inner = keys.shape[3]
    heads = inner // 64
    model = out_weight.shape[0]
    span = inner // X
    vmem = pltpu.VMEM

    def reduce_buffers():
        return [
            vmem((heads, 2, 32, answers), BF),
            vmem((heads, 32, answers), BF),
            vmem((heads, 32, answers), BF),
            vmem((Y - 1, Z, 32, answers), BF),
            vmem((Z, 32, answers), BF),
            vmem((Z - 1, 32, answers), BF),
        ]

    full = vmem((heads, 2, 32, answers), BF)
    scratch = [
        vmem((count, inner), BF),
        vmem((count, inner), BF),
        vmem((count, inner), BF),
        vmem((count, inner), BF),
        vmem((heads // 2, count, 2 * answers), BF),
        vmem((count, answers), F32),
        full, full, full, full,
        vmem((heads, 1, answers), F32),
        vmem((heads, 2, 32, answers), BF),
        vmem((heads, 2, answers), F32),
        vmem((heads, 32, answers), BF),
        vmem((heads, 2, answers), F32),
        vmem((heads, 32, answers), BF),
        vmem((heads, 2, answers), F32),
        vmem((Y - 1, Z, 32, answers), BF),
        vmem((Y - 1, Z, 2, answers), F32),
        vmem((Z, 32, answers), BF),
        vmem((Z, 2, answers), F32),
        vmem((Z - 1, 32, answers), BF),
        vmem((Z - 1, 2, answers), F32),
        vmem((heads, 2, 4, answers), F32),
        *reduce_buffers(),
        *reduce_buffers(),
        vmem((X, model, span), BF),
        vmem((X - 1, model, span), BF),
        vmem((X, model, span), BF),
    ]
    gather = (Z - 1) + (Y - 1) + Y
    scatter = Y + (Y - 1) + (Z - 1)
    copies = 4 * gather + 4 * scatter + 2 * (X - 1)
    scratch += [
        pltpu.SemaphoreType.DMA((copies,)),
        pltpu.SemaphoreType.DMA((copies,)),
        pltpu.SemaphoreType.DMA((2 * Y,)),
        pltpu.SemaphoreType.DMA((2 * Y,)),
    ]
    in_vmem = pl.BlockSpec(memory_space=pltpu.VMEM)
    in_place = pl.BlockSpec(memory_space=pl.ANY)
    layer_out, weight_grad, query_grad, key_grad, value_grad = pl.pallas_call(
        functools.partial(layer_kernel, (X, Y, Z, tokens)),
        out_shape=(
            jax.ShapeDtypeStruct((answers, model), BF),
            jax.ShapeDtypeStruct((model, inner), BF),
            jax.ShapeDtypeStruct((answers, queries.shape[2]), BF),
            jax.ShapeDtypeStruct((count, inner), BF),
            jax.ShapeDtypeStruct((count, inner), BF),
        ),
        in_specs=[
            in_vmem, in_place, in_place,
            pl.BlockSpec(memory_space=pltpu.SMEM),
            in_vmem, in_vmem,
        ],
        out_specs=(in_vmem, in_vmem, in_vmem, in_place, in_place),
        scratch_shapes=scratch,
        compiler_params=pltpu.CompilerParams(
            collective_id=0, has_side_effects=True, vmem_limit_bytes=56 << 20
        ),
    )(
        queries[0],
        keys.reshape(count, inner),
        values.reshape(count, inner),
        lengths,
        out_weight,
        out_cotangent[0],
    )
    return (
        layer_out[None],
        weight_grad.astype(F32),
        query_grad[None],
        key_grad.reshape(keys.shape),
        value_grad.reshape(values.shape),
    )


def solution(mesh):
    body = functools.partial(per_device, GRIDS[mesh.shape["psg"]], mesh.shape["dp"])
    return jax.shard_map(
        body,
        mesh=mesh,
        in_specs=(
            P("dp", None, "psg"),
            P("dp", "psg", None, None),
            P("dp", "psg", None, None),
            P("dp", "psg"),
            P("psg", None),
            P("dp", None, "psg"),
        ),
        out_specs=(
            P("dp", None, "psg"),
            P("psg", None),
            P("dp", None, "psg"),
            P("dp", "psg", None, None),
            P("dp", "psg", None, None),
        ),
        check_vma=False,
    )
```

time: 806 us -> 92.9 us (0.12)
  blocking collectives: 557 us -> 0 us
  waiting for transfers between devices: 145 us -> 0 us
  Pallas kernels: 0 us -> 79.8 us
  local copies, waits for them, and re-layouts: 43.2 us -> 10.4 us
  matrix products: 31 us -> 0 us
  between operations: 13.9 us -> 0.64 us
  other arithmetic: 10.5 us -> 1.78 us
    psum x1 -> x0, blocking collectives: 259 us -> none  [per_device(): lax.psum((jnp.sum(weights, axis=3), weighted_values(weights, value_heads)...]
    pmax x1 -> x0, blocking collectives: 243 us -> none  [per_device(): row_max = lax.pmax(local_max, 'psg')]
    reduce_scatter x1 -> x0, waiting for transfers between devices: 139 us -> none  [per_device(): lax.psum_scatter(query_terms, 'psg', scatter_dimension=2, tiled=True)]
    pallas_call x0 -> x1, Pallas kernels: none -> 79.8 us  [per_device(): pl.pallas_call(functools.partial(layer_kernel, (X, Y, Z, tokens)), out_sh...]
    all_gather x1 -> x0, blocking collectives: 54.9 us -> none  [per_device(): query_full = lax.all_gather(queries, 'psg', axis=2, tiled=True)]
    dot_general x9 -> x0, matrix products: 31 us -> none  [the longest x1 5.79 us: per_device(): jnp.einsum('bihe,bkhe->bhik', grad_heads, value_heads, preferred_element_...]
    unnamed x24 -> x8, local copies, waits for them, and re-layouts: 23.2 us -> 10.4 us
  transfers between devices with their start and end apart: 3 -> 0, of which waited for: 2 -> 0; matrix products, arithmetic and copies ran while one was open for 6% -> 0% of each run, Pallas kernels for 0% -> 0%
where the time goes in v1:
time: 92.9 us; the launch traced here: 92.6 us
  Pallas kernels  79.8 us (86%)
  local copies, waits for them, and re-layouts  10.4 us (11%)
  other arithmetic  1.78 us (2%)
    pallas_call x1, Pallas kernels, per_device(): pl.pallas_call(functools.partial(layer_kernel, (X, Y, Z, tokens)), out_sh...  79.8 us
    unnamed x8, local copies, waits for them, and re-layouts  10.4 us

profile of v1, /device:TPU:1, one launch (start us, length us, event | category | flops | bytes accessed | tf_op | source)
XLA Modules:
  0.0 92.6 jit_solution(9941234504108908201)
XLA Ops:
  0.6 1.4 %copy.11 = bf16[1,128,32]{2,1,0:T(8,128)(2,1)} copy(bf16[1,128,32]{1,2,0:T(8,128)(2,1)} %param.6) | data formatting | bytes 16384 | tf_op args[0]
  2.0 1.4 %copy.12 = bf16[1,128,64]{2,1,0:T(8,128)(2,1)} copy(bf16[1,128,64]{1,2,0:T(8,128)(2,1)} %param.11) | data formatting | bytes 32768 | tf_op args[5]
  3.5 79.8 %shard_map.101 = (bf16[128,64]{1,0:T(8,128)(2,1)}, bf16[64,2048]{1,0:T(8,128)(2,1)}, bf16[128,32]{1,0:T(8,128)(2,1)}, bf16[512,2048]{1,0:T(8,128)(2,1)}, bf16[512,2048]{1,0:T(8,128)(2,1)}) custom-call(bf16[128,32]{1,0:T(8,128)(2,1)} %bitcast.12, bf16[512,2048]{1,0:T(8,128)(2,1)} %bitcast.8, bf16[512,2048]{1,0:T(8,128)(2,1)} %bitcast.9, s32[1,2]{1,0:T(1,128)} %len_ref.1, ...), custom_call_target="tpu_custom_call" | custom-call | tf_op jit(solution)/shard_map/pallas_call | solution.py:447
  83.3 1.8 %convert_element_type.3 = f32[64,2048]{1,0:T(8,128)} convert(bf16[64,2048]{1,0:T(8,128)(2,1)} %get-tuple-element.11) | non-fusion elementwise | flops 131072 | bytes 786432 | tf_op jit(solution)/shard_map/convert_element_type | solution.py:476
  85.1 1.4 %copy.13 = bf16[1,128,64]{1,2,0:T(8,128)(2,1)} copy(bf16[1,128,64]{2,1,0:T(8,128)(2,1)} %bitcast.15) | data formatting | bytes 32768
  86.5 1.4 %copy.14 = bf16[1,128,32]{1,2,0:T(8,128)(2,1)} copy(bf16[1,128,32]{2,1,0:T(8,128)(2,1)} %bitcast.14) | data formatting | bytes 16384
  88.0 0.0 copy-start
  88.0 3.3 %copy.17 = bf16[1,2,256,2048]{3,2,1,0:T(8,128)(2,1)} copy(bf16[1,2,256,2048]{3,2,1,0:T(8,128)(2,1)} %bitcast.11) | data formatting | bytes 4194304
  91.3 0.0 copy-done
  91.3 1.3 %copy.18 = bf16[1,2,256,2048]{3,2,1,0:T(8,128)(2,1)} copy(bf16[1,2,256,2048]{3,2,1,0:T(8,128)(2,1)S(1)} %bitcast.10) | data formatting | bytes 4194304
Async XLA Ops:
  88.0 3.3 %copy-start = (bf16[512,2048]{1,0:T(8,128)(2,1)S(1)}, bf16[512,2048]{1,0:T(8,128)(2,1)}, u32[]{:S(2)}) copy-start(bf16[512,2048]{1,0:T(8,128)(2,1)} %get-tuple-element.14) | copy-start | bytes 6291460

commit v2 on v1

v2 whole, which is shorter than its diff:
```python
import functools

import jax
import jax.numpy as jnp
from jax import lax
from jax.experimental import pallas as pl
from jax.experimental.pallas import tpu as pltpu
from jax.sharding import PartitionSpec as P

BF = jnp.bfloat16
F32 = jnp.float32
MESH = pl.DeviceIdType.MESH
MASKED = -1e30
GRIDS = {64: (4, 8), 8: (2, 2)}

NN = (((1,), (0,)), ((), ()))
NT = (((1,), (1,)), ((), ()))
TN = (((0,), (0,)), ((), ()))


def dot(a, b, dims=NN):
    return lax.dot_general(a, b, dims, preferred_element_type=F32)


def block_diagonal(pair):
    zero = jnp.zeros((64, pair.shape[1]), pair.dtype)
    first = jnp.concatenate([pair[:64], zero], axis=0)
    second = jnp.concatenate([zero, pair[64:]], axis=0)
    return jnp.concatenate([first, second], axis=1)


class Wires:
    def __init__(self, send_sems, recv_sems):
        self.send_sems, self.recv_sems = send_sems, recv_sems
        self.count = 0
        self.sent = []

    def send(self, src, dst, device_id):
        copy = pltpu.make_async_remote_copy(
            src_ref=src,
            dst_ref=dst,
            send_sem=self.send_sems.at[self.count],
            recv_sem=self.recv_sems.at[self.count],
            device_id=device_id,
            device_id_type=MESH,
        )
        self.count += 1
        copy.start()
        self.sent.append(copy)
        return copy

    def finish(self):
        for copy in self.sent:
            copy.wait_send()


def layer_kernel(
    dims,
    q_hbm, k_hbm, v_hbm, len_ref, w_hbm, g_hbm,
    lo_ref, wg_ref, dq_ref, dkb, dvb,
    w_ref, g_ref, kb, vb, pb, ub, bias,
    qb, gb, cb, fgb, fqb, fdb, ab, bb, cen,
    po, st, rco, rcs, tbo, tbs, ryo, rys, tzo, tzs, rzo, rzs, sg,
    pg, rcg, tbg, ryg, tzg, rzg,
    pd, rcd, tbd, ryd, tzd, rzd,
    wgp, rxw, wgf,
    send_sems, recv_sems, load_sems,
):
    X, Y, Z, tokens = dims
    heads = Y * Z
    keys = kb.shape[0]
    answers = qb.shape[3]
    width = Z * 64
    x = lax.axis_index("dp")
    me = lax.axis_index("psg")
    c = lax.rem(me, 2)
    chip = me // 2
    z = lax.rem(chip, Z)
    y = chip // Z

    def at_yz(dy, dz):
        return {"psg": (lax.rem(y + dy, Y) * Z + lax.rem(z + dz, Z)) * 2 + c}

    def at_z(k):
        return at_yz(0, k)

    def at_y(k):
        return at_yz(k, 0)

    def at_x(k):
        return {"dp": lax.rem(x + k, X)}

    def hops(dy, dz):
        return min(dy, Y - dy) + min(dz, Z - dz)

    far_first = sorted(
        [(dy, dz) for dy in range(Y) for dz in range(Z) if (dy, dz) != (0, 0)],
        key=lambda d: -hops(*d),
    )
    near_rows = sorted(range(Y), key=lambda dy: min(dy, Y - dy))
    partner = {"psg": chip * 2 + (1 - c)}
    wires = Wires(send_sems, recv_sems)

    def block_of(k):
        return lax.rem(y + k, Y)

    def rows(b):
        return pl.ds(b * Z, Z)

    def lanes(b):
        return pl.ds(pl.multiple_of(b * width, width), width)

    barrier = pltpu.get_barrier_semaphore()
    peers = [at_yz(*d) for d in far_first] + [partner] + [at_x(k) for k in range(1, X)]
    for peer in peers:
        pl.semaphore_signal(barrier, inc=1, device_id=peer, device_id_type=MESH)

    small = []
    for n, (src, dst) in enumerate(((q_hbm, qb.at[chip, c]), (g_hbm, g_ref), (w_hbm, w_ref))):
        copy = pltpu.make_async_copy(src, dst, load_sems.at[2 * Y + n])
        copy.start()
        small.append(copy)
    loads = []
    for i in range(Y):
        b = block_of(i + 1)
        pair = []
        for n, (src, dst) in enumerate(((k_hbm, kb), (v_hbm, vb))):
            copy = pltpu.make_async_copy(
                src.at[:, lanes(b)], dst.at[:, lanes(b)], load_sems.at[2 * i + n]
            )
            copy.start()
            pair.append(copy)
        loads.append(pair)
    for copy in small:
        copy.wait()
    g_t = g_ref[...]
    pl.semaphore_wait(barrier, len(peers))

    def gather_start(buf):
        own = buf.at[chip, c]
        return {d: wires.send(own, own, at_yz(*d)) for d in far_first}

    def gather_core(buf, copies):
        core_copies = []
        for dy in near_rows:
            for dz in range(Z):
                if (dy, dz) in copies:
                    copies[dy, dz].wait_recv()
            part = buf.at[rows(block_of(Y - dy)), c]
            core_copies.append(wires.send(part, part, partner))
        return core_copies

    def gather_end(core_copies):
        for copy in core_copies:
            copy.wait_recv()

    def scatter_core(part, landing, b):
        return wires.send(part.at[rows(b), 1 - c], landing.at[rows(b)], partner)

    def scatter_y(part, landing, total, landing_y, copy, b, k):
        copy.wait_recv()
        both = part[rows(b), c].astype(F32) + landing[rows(b)].astype(F32)
        total[rows(b)] = both.astype(BF)
        if k < Y:
            return wires.send(total.at[rows(b)], landing_y.at[k - 1], at_y(k))
        return None

    def scatter_z(total, landing_y, total_z, landing_z, copies):
        both = total[rows(y)].astype(F32)
        for k in range(1, Y):
            copies[k - 1].wait_recv()
            both = both + landing_y[k - 1].astype(F32)
        total_z[...] = both.astype(BF)
        return [
            wires.send(total_z.at[lax.rem(z + k, Z)], landing_z.at[k - 1], at_z(k))
            for k in range(1, Z)
        ]

    def scatter_end(total_z, landing_z, copies):
        both = total_z[z].astype(F32)
        for k in range(1, Z):
            copies[k - 1].wait_recv()
            both = both + landing_z[k - 1].astype(F32)
        return both

    q_copies = gather_start(qb)
    g_core = []
    for i in range(Y):
        b = block_of(i + 1)
        term = dot(w_ref[:, lanes(b)], g_t, TN)
        pg[rows(b)] = term.reshape(Z, 2, 32, answers).astype(BF)
        g_core.append(scatter_core(pg, rcg, b))
    for passage in range(keys // tokens):
        position = lax.broadcasted_iota(jnp.int32, (tokens, answers), 0)
        bias[passage * tokens : (passage + 1) * tokens] = jnp.where(
            position < len_ref[0, passage], 0.0, MASKED
        )
    g_y = []
    for i in range(Y):
        g_y.append(scatter_y(pg, rcg, tbg, ryg, g_core[i], block_of(i + 1), i + 1))
    q_core = gather_core(qb, q_copies)
    g_z = scatter_z(tbg, ryg, tzg, rzg, g_y)
    gather_end(q_core)

    def columns(j):
        return pl.ds(pl.multiple_of(j * 128, 128), 128)

    def pair_of(buf, j):
        return block_diagonal(buf[pl.ds(2 * j, 2)].reshape(128, answers))

    def forward_pair(j):
        scores = dot(kb[:, columns(j)], pair_of(qb, j))
        for half in range(2):
            part = scores[:, half * answers : (half + 1) * answers] + bias[...]
            top = jnp.max(part, axis=0, keepdims=True)
            weights = jnp.exp(part - top)
            st[2 * j + half, 0:1, :] = top
            st[2 * j + half, 1:2, :] = jnp.sum(weights, axis=0, keepdims=True)
            pb[j, :, half * answers : (half + 1) * answers] = weights.astype(BF)
        out = dot(vb[:, columns(j)], pb[j], TN)
        po[2 * j] = out[:64, :answers].reshape(2, 32, answers).astype(BF)
        po[2 * j + 1] = out[64:, answers:].reshape(2, 32, answers).astype(BF)

    def run_block(body, b):
        @pl.loop(0, Z // 2)
        def _(i):
            body(b * (Z // 2) + i)

    def merge(terms):
        top = terms[0][1]
        for _, other, _ in terms[1:]:
            top = jnp.maximum(top, other)
        output, total = None, None
        for out, own, part in terms:
            scale = jnp.exp(own - top)
            output = out * scale if output is None else output + out * scale
            total = part * scale if total is None else total + part * scale
        return output, top, total

    def triple(out, stats):
        return out.astype(F32), stats[..., 0:1, :], stats[..., 1:2, :]

    def output_core(b):
        return scatter_core(po, rco, b), wires.send(st.at[rows(b)], rcs.at[rows(b)], partner)

    def output_y(copies, b, k):
        for copy in copies:
            copy.wait_recv()
        output, top, total = merge(
            [triple(po[rows(b), c], st[rows(b)]), triple(rco[rows(b)], rcs[rows(b)])]
        )
        tbo[rows(b)] = output.astype(BF)
        tbs[rows(b), 0:1, :] = top
        tbs[rows(b), 1:2, :] = total
        if k == Y:
            return None
        return (
            wires.send(tbo.at[rows(b)], ryo.at[k - 1], at_y(k)),
            wires.send(tbs.at[rows(b)], rys.at[k - 1], at_y(k)),
        )

    def output_z():
        terms = [triple(tbo[rows(y)], tbs[rows(y)])]
        for k in range(1, Y):
            for copy in o_y[k - 1]:
                copy.wait_recv()
            terms.append(triple(ryo[k - 1], rys[k - 1]))
        output, top, total = merge(terms)
        tzo[...] = output.astype(BF)
        tzs[:, 0:1, :] = top
        tzs[:, 1:2, :] = total
        copies = []
        for k in range(1, Z):
            t = lax.rem(z + k, Z)
            copies.append(
                (
                    wires.send(tzo.at[t], rzo.at[k - 1], at_z(k)),
                    wires.send(tzs.at[t], rzs.at[k - 1], at_z(k)),
                )
            )
        return copies

    def output_end(copies):
        terms = [triple(tzo[z], tzs[z])]
        for k in range(1, Z):
            for copy in copies[k - 1]:
                copy.wait_recv()
            terms.append(triple(rzo[k - 1], rzs[k - 1]))
        return merge(terms)

    def middle_pair(j):
        centers = []
        for half in range(2):
            h = 2 * j + half
            products = gb[h].astype(F32) * po[h].astype(F32)
            center = jnp.sum(products.reshape(64, answers), axis=0, keepdims=True) / st[h, 1:2, :]
            cen[h] = center
            centers.append(center)
        prob_grad = dot(vb[:, columns(j)], pair_of(gb, j))
        weights = pb[j]
        centered = prob_grad - jnp.concatenate(centers, axis=1)
        score_grad = (weights.astype(F32) * centered).astype(BF)
        ub[j] = score_grad
        key_pair = kb[:, columns(j)]
        for out, terms in ((ab, score_grad), (bb, weights)):
            product = dot(key_pair, terms, TN)
            out[2 * j] = product[:64, :answers]
            out[2 * j + 1] = product[64:, answers:]

    o_core, o_y = [], []
    for i in range(Y):
        b = block_of(i + 1)
        for copy in loads[i]:
            copy.wait()
        run_block(forward_pair, b)
        o_core.append(output_core(b))
        if i > 0:
            o_y.append(output_y(o_core[i - 1], block_of(i), i))
        if i == 0:
            gb[chip, c] = scatter_end(tzg, rzg, g_z).astype(BF)
            g_copies = gather_start(gb)
    output_y(o_core[Y - 1], y, Y)
    o_z = output_z()
    gather_end(gather_core(gb, g_copies))
    for b in range(Y - 1):
        run_block(middle_pair, b)

    output, top, total = output_end(o_z)
    context = (output / total).astype(BF)
    cb[chip, c] = context
    sg[chip, c, 0:1, :] = top
    sg[chip, c, 1:2, :] = total
    sg[chip, c, 2:3, :] = jnp.sum(
        gb[chip, c].astype(F32) * context.astype(F32), axis=0, keepdims=True
    )
    sg[chip, c, 3:4, :] = total
    s_copies = gather_start(sg)
    c_copies = gather_start(cb)
    run_block(middle_pair, Y - 1)
    s_core = gather_core(sg, s_copies)
    gather_end(s_core)

    d_core = []
    for i in range(Y):
        b = block_of(i + 1)
        stats = sg[rows(b)]
        factor = jnp.exp(st[rows(b), 0:1, :] - stats[:, 0, 0:1, :]) / stats[:, 0, 1:2, :]
        shift = factor * (stats[:, 0, 2:3, :] + stats[:, 1, 2:3, :] - cen[rows(b)])
        query_terms = factor * ab[rows(b)] - shift * bb[rows(b)]
        pd[rows(b)] = query_terms.astype(BF).reshape(Z, 2, 32, answers)
        d_core.append(scatter_core(pd, rcd, b))

        def scaled(buf, by):
            wide = buf[rows(b)].astype(F32).reshape(Z, 64, answers) * by
            return wide.astype(BF).reshape(Z, 2, 32, answers)

        fgb[rows(b)] = scaled(gb, factor)
        fqb[rows(b)] = scaled(qb, factor)
        fdb[rows(b)] = scaled(qb, -shift)

    def backward_pair(j):
        both = jnp.concatenate([pair_of(fgb, j), pair_of(fdb, j)], axis=0)
        from_weights = dot(pb[j], both, NT)
        dvb[:, columns(j)] = from_weights[:, :128].astype(BF)
        key_grad = from_weights[:, 128:] + dot(ub[j], pair_of(fqb, j), NT)
        dkb[:, columns(j)] = key_grad.astype(BF)

    span = heads * 64 // X
    d_y = []
    for i in range(Y):
        d_y.append(scatter_y(pd, rcd, tbd, ryd, d_core[i], block_of(i + 1), i + 1))
    c_core = gather_core(cb, c_copies)
    run_block(backward_pair, 0)
    gather_end(c_core)
    everything = cb[...].reshape(heads * 64, answers)
    for n in range(X):
        wgp[n] = dot(g_t, everything[n * span : (n + 1) * span], NT).astype(BF)
    w_copies = [
        wires.send(wgp.at[lax.rem(x + k, X)], rxw.at[k - 1], at_x(k)) for k in range(1, X)
    ]
    d_z = scatter_z(tbd, ryd, tzd, rzd, d_y)
    lo_ref[...] = dot(w_ref[...], everything).astype(BF)
    for b in range(1, Y - 1):
        run_block(backward_pair, b)
    both = wgp[x].astype(F32)
    for k in range(1, X):
        w_copies[k - 1].wait_recv()
        both = both + rxw[k - 1].astype(F32)
    wgf[x] = both.astype(BF)
    w_copies = [wires.send(wgf.at[x], wgf.at[x], at_x(k)) for k in range(1, X)]
    run_block(backward_pair, Y - 1)
    dq_ref[...] = scatter_end(tzd, rzd, d_z).astype(BF)
    wires.finish()
    for copy in w_copies:
        copy.wait_recv()
    for n in range(X):
        wg_ref[:, n * span : (n + 1) * span] = wgf[n].astype(F32)


def store_kernel(*refs):
    count = (len(refs) - 1) // 2
    copies = [
        pltpu.make_async_copy(refs[n], refs[count + n], refs[-1].at[n]) for n in range(count)
    ]
    for copy in copies:
        copy.start()
    for copy in copies:
        copy.wait()


def per_device(grid, chips_x, queries, keys, values, lengths, out_weight, out_cotangent):
    Y, Z = grid
    X = chips_x
    answers = queries.shape[1]
    tokens = keys.shape[2]
    count = keys.shape[1] * tokens
    inner = keys.shape[3]
    heads = inner // 64
    model = out_weight.shape[0]
    span = inner // X
    vmem = pltpu.VMEM

    def reduce_buffers():
        return [
            vmem((heads, 2, 32, answers), BF),
            vmem((heads, 32, answers), BF),
            vmem((heads, 32, answers), BF),
            vmem((Y - 1, Z, 32, answers), BF),
            vmem((Z, 32, answers), BF),
            vmem((Z - 1, 32, answers), BF),
        ]

    full = vmem((heads, 2, 32, answers), BF)
    scratch = [
        vmem((model, inner), BF),
        vmem((model, answers), BF),
        vmem((count, inner), BF),
        vmem((count, inner), BF),
        vmem((heads // 2, count, 2 * answers), BF),
        vmem((heads // 2, count, 2 * answers), BF),
        vmem((count, answers), F32),
        full, full, full, full, full, full,
        vmem((heads, 64, answers), F32),
        vmem((heads, 64, answers), F32),
        vmem((heads, 1, answers), F32),
        vmem((heads, 2, 32, answers), BF),
        vmem((heads, 2, answers), F32),
        vmem((heads, 32, answers), BF),
        vmem((heads, 2, answers), F32),
        vmem((heads, 32, answers), BF),
        vmem((heads, 2, answers), F32),
        vmem((Y - 1, Z, 32, answers), BF),
        vmem((Y - 1, Z, 2, answers), F32),
        vmem((Z, 32, answers), BF),
        vmem((Z, 2, answers), F32),
        vmem((Z - 1, 32, answers), BF),
        vmem((Z - 1, 2, answers), F32),
        vmem((heads, 2, 4, answers), F32),
        *reduce_buffers(),
        *reduce_buffers(),
        vmem((X, model, span), BF),
        vmem((X - 1, model, span), BF),
        vmem((X, model, span), BF),
    ]
    gather = heads - 1 + Y
    scatter = Y + (Y - 1) + (Z - 1)
    copies = 4 * gather + 4 * scatter + 2 * (X - 1)
    scratch += [
        pltpu.SemaphoreType.DMA((copies,)),
        pltpu.SemaphoreType.DMA((copies,)),
        pltpu.SemaphoreType.DMA((2 * Y + 3,)),
    ]
    in_vmem = pl.BlockSpec(memory_space=pltpu.VMEM)
    in_hbm = pl.BlockSpec(memory_space=pltpu.HBM)
    shapes = (
        ((model, answers), BF),
        ((model, inner), F32),
        ((queries.shape[2], answers), BF),
        ((count, inner), BF),
        ((count, inner), BF),
    )
    results = pl.pallas_call(
        functools.partial(layer_kernel, (X, Y, Z, tokens)),
        out_shape=tuple(vmem(*shape) for shape in shapes),
        in_specs=[
            in_hbm, in_hbm, in_hbm,
            pl.BlockSpec(memory_space=pltpu.SMEM),
            in_hbm, in_hbm,
        ],
        out_specs=(in_vmem,) * len(shapes),
        scratch_shapes=scratch,
        compiler_params=pltpu.CompilerParams(
            collective_id=0, has_side_effects=True, vmem_limit_bytes=50 << 20
        ),
    )(
        queries[0].T,
        keys.reshape(count, inner),
        values.reshape(count, inner),
        lengths,
        out_weight,
        out_cotangent[0].T,
    )
    layer_out, weight_grad, query_grad, key_grad, value_grad = pl.pallas_call(
        store_kernel,
        out_shape=tuple(jax.ShapeDtypeStruct(*shape) for shape in shapes),
        in_specs=[in_vmem] * len(shapes),
        out_specs=(in_hbm,) * len(shapes),
        scratch_shapes=[pltpu.SemaphoreType.DMA((len(shapes),))],
        compiler_params=pltpu.CompilerParams(vmem_limit_bytes=4 << 20),
    )(*(pltpu.with_memory_space_constraint(part, pltpu.VMEM) for part in results))
    return (
        layer_out.T[None],
        weight_grad,
        query_grad.T[None],
        key_grad.reshape(keys.shape),
        value_grad.reshape(values.shape),
    )


def solution(mesh):
    body = functools.partial(per_device, GRIDS[mesh.shape["psg"]], mesh.shape["dp"])
    return jax.shard_map(
        body,
        mesh=mesh,
        in_specs=(
            P("dp", None, "psg"),
            P("dp", "psg", None, None),
            P("dp", "psg", None, None),
            P("dp", "psg"),
            P("psg", None),
            P("dp", None, "psg"),
        ),
        out_specs=(
            P("dp", None, "psg"),
            P("psg", None),
            P("dp", None, "psg"),
            P("dp", "psg", None, None),
            P("dp", "psg", None, None),
        ),
        check_vma=False,
    )
```

time: 92.9 us -> 72 us (0.78)
  local copies, waits for them, and re-layouts: 10.4 us -> 0 us
  Pallas kernels: 79.8 us -> 71.2 us
  other arithmetic: 1.78 us -> 0 us
    pallas_call x1, Pallas kernels: 79.8 us -> 69 us  [per_device(): pl.pallas_call(functools.partial(layer_kernel, (X, Y, Z, tokens)), out_sh...]
    unnamed x8 -> x0, local copies, waits for them, and re-layouts: 10.4 us -> none
    pallas_call x0 -> x1, Pallas kernels: none -> 2.24 us  [per_device(): pl.pallas_call(store_kernel, out_shape=tuple((jax.ShapeDtypeStruct(*shape...]
    convert_element_type x1 -> x0, other arithmetic: 1.78 us -> none  [per_device(): weight_grad.astype(F32)]
where the time goes in v2:
time: 72 us; the launch traced here: 71.9 us
  Pallas kernels  71.2 us (99%)
    pallas_call x1, Pallas kernels, per_device(): pl.pallas_call(functools.partial(layer_kernel, (X, Y, Z, tokens)), out_sh...  69 us
    pallas_call x1, Pallas kernels, per_device(): pl.pallas_call(store_kernel, out_shape=tuple((jax.ShapeDtypeStruct(*shape...  2.24 us

profile of v2, /device:TPU:1, one launch (start us, length us, event | category | flops | bytes accessed | tf_op | source)
XLA Modules:
  0.0 71.9 jit_solution(13241206424482475491)
XLA Ops:
  0.6 69.0 %shard_map.101 = (bf16[64,128]{1,0:T(8,128)(2,1)S(1)}, f32[64,2048]{1,0:T(8,128)S(1)}, bf16[32,128]{1,0:T(8,128)(2,1)S(1)}, bf16[512,2048]{1,0:T(8,128)(2,1)S(1)}, bf16[512,2048]{1,0:T(8,128)(2,1)S(1)}) custom-call(bf16[32,128]{1,0:T(8,128)(2,1)} %bitcast.19, bf16[512,2048]{1,0:T(8,128)(2,1)} %bitcast.16, bf16[512,2048]{1,0:T(8,128)(2,1)} %bitcast.17, ...), custom_call_target="tpu_custom_call" | custom-call | tf_op jit(solution)/shard_map/pallas_call | solution.py:482
  69.6 2.2 %shard_map.102 = (bf16[64,128]{1,0:T(8,128)(2,1)}, f32[64,2048]{1,0:T(8,128)}, bf16[32,128]{1,0:T(8,128)(2,1)}, bf16[512,2048]{1,0:T(8,128)(2,1)}, bf16[512,2048]{1,0:T(8,128)(2,1)}) custom-call(bf16[64,128]{1,0:T(8,128)(2,1)S(1)} %get-tuple-element.15.refs_0_, f32[64,2048]{1,0:T(8,128)S(1)} %get-tuple-element.16.refs_1_, ...), custom_call_target="tpu_custom_call" | custom-call | tf_op jit(solution)/shard_map/pallas_call | solution.py:503

commit v3 on v2

--- a/solution.py
+++ b/solution.py
@@ -49,9 +49,11 @@
         self.sent.append(copy)
         return copy
 
-    def finish(self):
-        for copy in self.sent:
+    def finish(self, keep=0):
+        count = len(self.sent) - keep
+        for copy in self.sent[:count]:
             copy.wait_send()
+        self.sent = self.sent[count:]
 
 
 def layer_kernel(
@@ -61,8 +63,8 @@
     w_ref, g_ref, kb, vb, pb, ub, bias,
     qb, gb, cb, fgb, fqb, fdb, ab, bb, cen,
     po, st, rco, rcs, tbo, tbs, ryo, rys, tzo, tzs, rzo, rzs, sg,
-    pg, rcg, tbg, ryg, tzg, rzg,
-    pd, rcd, tbd, ryd, tzd, rzd,
+    pg, rcg, tbg, rzg,
+    pd, rcd, tbd, rzd,
     wgp, rxw, wgf,
     send_sems, recv_sems, load_sems,
 ):
@@ -90,14 +92,12 @@
     def at_x(k):
         return {"dp": lax.rem(x + k, X)}
 
-    def hops(dy, dz):
-        return min(dy, Y - dy) + min(dz, Z - dz)
-
-    far_first = sorted(
-        [(dy, dz) for dy in range(Y) for dz in range(Z) if (dy, dz) != (0, 0)],
-        key=lambda d: -hops(*d),
-    )
-    near_rows = sorted(range(Y), key=lambda dy: min(dy, Y - dy))
+    targets = [
+        (dy, dz)
+        for dy in reversed(range(Y))
+        for dz in sorted(range(Z), key=lambda dz: -min(dz, Z - dz))
+        if (dy, dz) != (0, 0)
+    ]
     partner = {"psg": chip * 2 + (1 - c)}
     wires = Wires(send_sems, recv_sems)
 
@@ -111,7 +111,7 @@
         return pl.ds(pl.multiple_of(b * width, width), width)
 
     barrier = pltpu.get_barrier_semaphore()
-    peers = [at_yz(*d) for d in far_first] + [partner] + [at_x(k) for k in range(1, X)]
+    peers = [at_yz(*d) for d in targets] + [partner] + [at_x(k) for k in range(1, X)]
     for peer in peers:
         pl.semaphore_signal(barrier, inc=1, device_id=peer, device_id_type=MESH)
 
@@ -138,17 +138,17 @@
 
     def gather_start(buf):
         own = buf.at[chip, c]
-        return {d: wires.send(own, own, at_yz(*d)) for d in far_first}
+        return {d: wires.send(own, own, at_yz(*d)) for d in targets}
+
+    def gather_block(buf, copies, i):
+        for dz in range(Z):
+            if (Y - 1 - i, dz) in copies:
+                copies[Y - 1 - i, dz].wait_recv()
+        part = buf.at[rows(block_of(i + 1)), c]
+        return wires.send(part, part, partner)
 
     def gather_core(buf, copies):
-        core_copies = []
-        for dy in near_rows:
-            for dz in range(Z):
-                if (dy, dz) in copies:
-                    copies[dy, dz].wait_recv()
-            part = buf.at[rows(block_of(Y - dy)), c]
-            core_copies.append(wires.send(part, part, partner))
-        return core_copies
+        return [gather_block(buf, copies, i) for i in range(Y)]
 
     def gather_end(core_copies):
         for copy in core_copies:
@@ -157,31 +157,26 @@
     def scatter_core(part, landing, b):
         return wires.send(part.at[rows(b), 1 - c], landing.at[rows(b)], partner)
 
-    def scatter_y(part, landing, total, landing_y, copy, b, k):
-        copy.wait_recv()
-        both = part[rows(b), c].astype(F32) + landing[rows(b)].astype(F32)
-        total[rows(b)] = both.astype(BF)
-        if k < Y:
-            return wires.send(total.at[rows(b)], landing_y.at[k - 1], at_y(k))
-        return None
-
-    def scatter_z(total, landing_y, total_z, landing_z, copies):
-        both = total[rows(y)].astype(F32)
-        for k in range(1, Y):
-            copies[k - 1].wait_recv()
-            both = both + landing_y[k - 1].astype(F32)
-        total_z[...] = both.astype(BF)
-        return [
-            wires.send(total_z.at[lax.rem(z + k, Z)], landing_z.at[k - 1], at_z(k))
-            for k in range(1, Z)
-        ]
-
-    def scatter_end(total_z, landing_z, copies):
-        both = total_z[z].astype(F32)
-        for k in range(1, Z):
-            copies[k - 1].wait_recv()
-            both = both + landing_z[k - 1].astype(F32)
-        return both
+    def scatter_start(part, landing, total, pieces, core_copies):
+        copies = []
+        for i in range(Y):
+            b = block_of(i + 1)
+            core_copies[i].wait_recv()
+            both = part[rows(b), c].astype(F32) + landing[rows(b)].astype(F32)
+            total[rows(b)] = both.astype(BF)
+            dy = (i + 1) % Y
+            for dz in sorted(range(Z), key=lambda dz: -min(dz, Z - dz)):
+                if (dy, dz) != (0, 0):
+                    piece = total.at[b * Z + lax.rem(z + dz, Z)]
+                    copies.append(
+                        wires.send(piece, pieces.at[dy * Z + dz - 1], at_yz(dy, dz))
+                    )
+        return copies
+
+    def scatter_end(total, pieces, copies):
+        for copy in copies:
+            copy.wait_recv()
+        return total[chip].astype(F32) + jnp.sum(pieces[...].astype(F32), axis=0)
 
     q_copies = gather_start(qb)
     g_core = []
@@ -195,12 +190,7 @@
         bias[passage * tokens : (passage + 1) * tokens] = jnp.where(
             position < len_ref[0, passage], 0.0, MASKED
         )
-    g_y = []
-    for i in range(Y):
-        g_y.append(scatter_y(pg, rcg, tbg, ryg, g_core[i], block_of(i + 1), i + 1))
-    q_core = gather_core(qb, q_copies)
-    g_z = scatter_z(tbg, ryg, tzg, rzg, g_y)
-    gather_end(q_core)
+    g_pieces = scatter_start(pg, rcg, tbg, rzg, g_core)
 
     def columns(j):
         return pl.ds(pl.multiple_of(j * 128, 128), 128)
@@ -222,7 +212,7 @@
         po[2 * j + 1] = out[64:, answers:].reshape(2, 32, answers).astype(BF)
 
     def run_block(body, b):
-        @pl.loop(0, Z // 2)
+        @pl.loop(0, Z // 2, unroll=Z // 2)
         def _(i):
             body(b * (Z // 2) + i)
 
@@ -308,22 +298,23 @@
             out[2 * j + 1] = product[64:, answers:]
 
     o_core, o_y = [], []
+    q_core = [gather_block(qb, q_copies, 0)]
     for i in range(Y):
         b = block_of(i + 1)
+        if i + 1 < Y:
+            q_core.append(gather_block(qb, q_copies, i + 1))
         for copy in loads[i]:
             copy.wait()
+        q_core[i].wait_recv()
         run_block(forward_pair, b)
         o_core.append(output_core(b))
         if i > 0:
             o_y.append(output_y(o_core[i - 1], block_of(i), i))
-        if i == 0:
-            gb[chip, c] = scatter_end(tzg, rzg, g_z).astype(BF)
-            g_copies = gather_start(gb)
     output_y(o_core[Y - 1], y, Y)
     o_z = output_z()
-    gather_end(gather_core(gb, g_copies))
-    for b in range(Y - 1):
-        run_block(middle_pair, b)
+    gb[chip, c] = scatter_end(tbg, rzg, g_pieces).astype(BF)
+    g_copies = gather_start(gb)
+    older = len(wires.sent)
 
     output, top, total = output_end(o_z)
     context = (output / total).astype(BF)
@@ -336,11 +327,14 @@
     sg[chip, c, 3:4, :] = total
     s_copies = gather_start(sg)
     c_copies = gather_start(cb)
-    run_block(middle_pair, Y - 1)
+    gather_end(gather_core(gb, g_copies))
+    for b in range(Y):
+        run_block(middle_pair, b)
+    wires.finish(keep=len(wires.sent) - older)
     s_core = gather_core(sg, s_copies)
     gather_end(s_core)
 
-    d_core = []
+    factors, shifts, d_core = [], [], []
     for i in range(Y):
         b = block_of(i + 1)
         stats = sg[rows(b)]
@@ -349,14 +343,36 @@
         query_terms = factor * ab[rows(b)] - shift * bb[rows(b)]
         pd[rows(b)] = query_terms.astype(BF).reshape(Z, 2, 32, answers)
         d_core.append(scatter_core(pd, rcd, b))
+        factors.append(factor)
+        shifts.append(shift)
+
+    c_core = gather_core(cb, c_copies)
+    d_pieces = scatter_start(pd, rcd, tbd, rzd, d_core)
+
+    span = width // X
+    w_copies = []
+    for i in range(Y):
+        c_core[i].wait_recv()
+        term = dot(g_t, cb[rows(block_of(i + 1))].reshape(width, answers), NT).astype(BF)
+        for n in range(X):
+            wgp[i, n] = term[:, n * span : (n + 1) * span]
+        w_copies.append(
+            [
+                wires.send(wgp.at[i, lax.rem(x + k, X)], rxw.at[i, k - 1], at_x(k))
+                for k in range(1, X)
+            ]
+        )
+
+    for i in range(Y):
+        b = block_of(i + 1)
 
         def scaled(buf, by):
             wide = buf[rows(b)].astype(F32).reshape(Z, 64, answers) * by
             return wide.astype(BF).reshape(Z, 2, 32, answers)
 
-        fgb[rows(b)] = scaled(gb, factor)
-        fqb[rows(b)] = scaled(qb, factor)
-        fdb[rows(b)] = scaled(qb, -shift)
+        fgb[rows(b)] = scaled(gb, factors[i])
+        fqb[rows(b)] = scaled(qb, factors[i])
+        fdb[rows(b)] = scaled(qb, -shifts[i])
 
     def backward_pair(j):
         both = jnp.concatenate([pair_of(fgb, j), pair_of(fdb, j)], axis=0)
@@ -365,36 +381,29 @@
         key_grad = from_weights[:, 128:] + dot(ub[j], pair_of(fqb, j), NT)
         dkb[:, columns(j)] = key_grad.astype(BF)
 
-    span = heads * 64 // X
-    d_y = []
-    for i in range(Y):
-        d_y.append(scatter_y(pd, rcd, tbd, ryd, d_core[i], block_of(i + 1), i + 1))
-    c_core = gather_core(cb, c_copies)
-    run_block(backward_pair, 0)
-    gather_end(c_core)
-    everything = cb[...].reshape(heads * 64, answers)
-    for n in range(X):
-        wgp[n] = dot(g_t, everything[n * span : (n + 1) * span], NT).astype(BF)
-    w_copies = [
-        wires.send(wgp.at[lax.rem(x + k, X)], rxw.at[k - 1], at_x(k)) for k in range(1, X)
-    ]
-    d_z = scatter_z(tbd, ryd, tzd, rzd, d_y)
-    lo_ref[...] = dot(w_ref[...], everything).astype(BF)
-    for b in range(1, Y - 1):
+    for b in range(Y // 2):
         run_block(backward_pair, b)
-    both = wgp[x].astype(F32)
-    for k in range(1, X):
-        w_copies[k - 1].wait_recv()
-        both = both + rxw[k - 1].astype(F32)
-    wgf[x] = both.astype(BF)
-    w_copies = [wires.send(wgf.at[x], wgf.at[x], at_x(k)) for k in range(1, X)]
-    run_block(backward_pair, Y - 1)
-    dq_ref[...] = scatter_end(tzd, rzd, d_z).astype(BF)
+    sums = []
+    for i in range(Y):
+        b = block_of(i + 1)
+        both = wgp[i, x].astype(F32)
+        for k in range(1, X):
+            w_copies[i][k - 1].wait_recv()
+            both = both + rxw[i, k - 1].astype(F32)
+        wgf[b, x] = both.astype(BF)
+        sums += [wires.send(wgf.at[b, x], wgf.at[b, x], at_x(k)) for k in range(1, X)]
+    for b in range(Y // 2, Y):
+        run_block(backward_pair, b)
+    lo_ref[...] = dot(w_ref[...], cb[...].reshape(heads * 64, answers)).astype(BF)
+    wires.finish(keep=len(sums))
+    dq_ref[...] = scatter_end(tbd, rzd, d_pieces).astype(BF)
+    for copy in sums:
+        copy.wait_recv()
+    for b in range(Y):
+        for n in range(X):
+            at = (b * X + n) * span
+            wg_ref[:, at : at + span] = wgf[b, n].astype(F32)
     wires.finish()
-    for copy in w_copies:
-        copy.wait_recv()
-    for n in range(X):
-        wg_ref[:, n * span : (n + 1) * span] = wgf[n].astype(F32)
 
 
 def store_kernel(*refs):
@@ -417,7 +426,7 @@
     inner = keys.shape[3]
     heads = inner // 64
     model = out_weight.shape[0]
-    span = inner // X
+    span = inner // (X * Y)
     vmem = pltpu.VMEM
 
     def reduce_buffers():
@@ -425,9 +434,7 @@
             vmem((heads, 2, 32, answers), BF),
             vmem((heads, 32, answers), BF),
             vmem((heads, 32, answers), BF),
-            vmem((Y - 1, Z, 32, answers), BF),
-            vmem((Z, 32, answers), BF),
-            vmem((Z - 1, 32, answers), BF),
+            vmem((heads - 1, 32, answers), BF),
         ]
 
     full = vmem((heads, 2, 32, answers), BF)
@@ -458,13 +465,14 @@
         vmem((heads, 2, 4, answers), F32),
         *reduce_buffers(),
         *reduce_buffers(),
-        vmem((X, model, span), BF),
-        vmem((X - 1, model, span), BF),
-        vmem((X, model, span), BF),
+        vmem((Y, X, model, span), BF),
+        vmem((Y, X - 1, model, span), BF),
+        vmem((Y, X, model, span), BF),
     ]
     gather = heads - 1 + Y
-    scatter = Y + (Y - 1) + (Z - 1)
-    copies = 4 * gather + 4 * scatter + 2 * (X - 1)
+    scatter = Y + heads - 1
+    staged = Y + (Y - 1) + (Z - 1)
+    copies = 4 * gather + 2 * scatter + 2 * staged + 2 * Y * (X - 1)
     scratch += [
         pltpu.SemaphoreType.DMA((copies,)),
         pltpu.SemaphoreType.DMA((copies,)),

time: 72 us -> 65.2 us (0.906)
  Pallas kernels: 71.2 us -> 64.3 us
    pallas_call x1, Pallas kernels: 69 us -> 62.1 us  [per_device(): pl.pallas_call(functools.partial(layer_kernel, (X, Y, Z, tokens)), out_sh...]
where the time goes in v3:
time: 65.2 us; the launch traced here: 65.1 us
  Pallas kernels  64.3 us (99%)
  between operations  0.8 us (1%)
    pallas_call x1, Pallas kernels, per_device(): pl.pallas_call(functools.partial(layer_kernel, (X, Y, Z, tokens)), out_sh...  62.1 us
    pallas_call x1, Pallas kernels, per_device(): pl.pallas_call(store_kernel, out_shape=tuple((jax.ShapeDtypeStruct(*shape...  2.24 us

profile of v3, /device:TPU:1, one launch (start us, length us, event | category | flops | bytes accessed | tf_op | source)
XLA Modules:
  0.0 65.1 jit_solution(15133359015830910644)
XLA Ops:
  0.6 62.1 %shard_map.101 = (bf16[64,128]{1,0:T(8,128)(2,1)S(1)}, f32[64,2048]{1,0:T(8,128)S(1)}, bf16[32,128]{1,0:T(8,128)(2,1)S(1)}, bf16[512,2048]{1,0:T(8,128)(2,1)S(1)}, bf16[512,2048]{1,0:T(8,128)(2,1)S(1)}) custom-call(bf16[32,128]{1,0:T(8,128)(2,1)} %bitcast.19, bf16[512,2048]{1,0:T(8,128)(2,1)} %bitcast.16, bf16[512,2048]{1,0:T(8,128)(2,1)} %bitcast.17, ...), custom_call_target="tpu_custom_call" | custom-call | tf_op jit(solution)/shard_map/pallas_call | solution.py:490
  62.7 2.2 %shard_map.102 = (bf16[64,128]{1,0:T(8,128)(2,1)}, f32[64,2048]{1,0:T(8,128)}, bf16[32,128]{1,0:T(8,128)(2,1)}, bf16[512,2048]{1,0:T(8,128)(2,1)}, bf16[512,2048]{1,0:T(8,128)(2,1)}) custom-call(bf16[64,128]{1,0:T(8,128)(2,1)S(1)} %get-tuple-element.15.refs_0_, f32[64,2048]{1,0:T(8,128)S(1)} %get-tuple-element.16.refs_1_, ...), custom_call_target="tpu_custom_call" | custom-call | tf_op jit(solution)/shard_map/pallas_call | solution.py:511

commit v4 on v3

--- a/solution.py
+++ b/solution.py
@@ -60,7 +60,7 @@
     dims,
     q_hbm, k_hbm, v_hbm, len_ref, w_hbm, g_hbm,
     lo_ref, wg_ref, dq_ref, dkb, dvb,
-    w_ref, g_ref, kb, vb, pb, ub, bias,
+    w_ref, g_ref, kb, vb, vt, pb, ub, bias,
     qb, gb, cb, fgb, fqb, fdb, ab, bb, cen,
     po, st, rco, rcs, tbo, tbs, ryo, rys, tzo, tzs, rzo, rzs, sg,
     pg, rcg, tbg, rzg,
@@ -207,7 +207,7 @@
             st[2 * j + half, 0:1, :] = top
             st[2 * j + half, 1:2, :] = jnp.sum(weights, axis=0, keepdims=True)
             pb[j, :, half * answers : (half + 1) * answers] = weights.astype(BF)
-        out = dot(vb[:, columns(j)], pb[j], TN)
+        out = dot(vt[columns(j), :], pb[j])
         po[2 * j] = out[:64, :answers].reshape(2, 32, answers).astype(BF)
         po[2 * j + 1] = out[64:, answers:].reshape(2, 32, answers).astype(BF)
 
@@ -298,22 +298,29 @@
             out[2 * j + 1] = product[64:, answers:]
 
     o_core, o_y = [], []
+    for pair in loads:
+        for copy in pair:
+            copy.wait()
+
+    @pl.loop(0, heads // 2, unroll=Z // 2)
+    def _(j):
+        vt[columns(j), :] = vb[:, columns(j)].T
+
     q_core = [gather_block(qb, q_copies, 0)]
     for i in range(Y):
         b = block_of(i + 1)
         if i + 1 < Y:
             q_core.append(gather_block(qb, q_copies, i + 1))
-        for copy in loads[i]:
-            copy.wait()
         q_core[i].wait_recv()
         run_block(forward_pair, b)
         o_core.append(output_core(b))
         if i > 0:
             o_y.append(output_y(o_core[i - 1], block_of(i), i))
+        if i == Y - 2:
+            gb[chip, c] = scatter_end(tbg, rzg, g_pieces).astype(BF)
+            g_copies = gather_start(gb)
     output_y(o_core[Y - 1], y, Y)
     o_z = output_z()
-    gb[chip, c] = scatter_end(tbg, rzg, g_pieces).astype(BF)
-    g_copies = gather_start(gb)
     older = len(wires.sent)
 
     output, top, total = output_end(o_z)
@@ -443,6 +450,7 @@
         vmem((model, answers), BF),
         vmem((count, inner), BF),
         vmem((count, inner), BF),
+        vmem((inner, count), BF),
         vmem((heads // 2, count, 2 * answers), BF),
         vmem((heads // 2, count, 2 * answers), BF),
         vmem((count, answers), F32),

time: 65.2 us -> 63.4 us (0.972)
  Pallas kernels: 64.3 us -> 62.6 us
    pallas_call x1, Pallas kernels: 62.1 us -> 60.4 us  [per_device(): pl.pallas_call(functools.partial(layer_kernel, (X, Y, Z, tokens)), out_sh...]
where the time goes in v4:
time: 63.4 us; the launch traced here: 63.3 us
  Pallas kernels  62.6 us (99%)
  between operations  0.64 us (1%)
    pallas_call x1, Pallas kernels, per_device(): pl.pallas_call(functools.partial(layer_kernel, (X, Y, Z, tokens)), out_sh...  60.4 us
    pallas_call x1, Pallas kernels, per_device(): pl.pallas_call(store_kernel, out_shape=tuple((jax.ShapeDtypeStruct(*shape...  2.24 us

profile of v4, /device:TPU:1, one launch (start us, length us, event | category | flops | bytes accessed | tf_op | source)
XLA Modules:
  0.0 63.3 jit_solution(5003213484081372572)
XLA Ops:
  0.6 60.4 %shard_map.101 = (bf16[64,128]{1,0:T(8,128)(2,1)S(1)}, f32[64,2048]{1,0:T(8,128)S(1)}, bf16[32,128]{1,0:T(8,128)(2,1)S(1)}, bf16[512,2048]{1,0:T(8,128)(2,1)S(1)}, bf16[512,2048]{1,0:T(8,128)(2,1)S(1)}) custom-call(bf16[32,128]{1,0:T(8,128)(2,1)} %bitcast.19, bf16[512,2048]{1,0:T(8,128)(2,1)} %bitcast.16, bf16[512,2048]{1,0:T(8,128)(2,1)} %bitcast.17, ...), custom_call_target="tpu_custom_call" | custom-call | tf_op jit(solution)/shard_map/pallas_call | solution.py:498
  61.0 2.2 %shard_map.102 = (bf16[64,128]{1,0:T(8,128)(2,1)}, f32[64,2048]{1,0:T(8,128)}, bf16[32,128]{1,0:T(8,128)(2,1)}, bf16[512,2048]{1,0:T(8,128)(2,1)}, bf16[512,2048]{1,0:T(8,128)(2,1)}) custom-call(bf16[64,128]{1,0:T(8,128)(2,1)S(1)} %get-tuple-element.15.refs_0_, f32[64,2048]{1,0:T(8,128)S(1)} %get-tuple-element.16.refs_1_, ...), custom_call_target="tpu_custom_call" | custom-call | tf_op jit(solution)/shard_map/pallas_call | solution.py:519
